TPU v7x, 256 devices: a whole 4x4x8 slice. The times are simulated.
256 devices in a mesh: sec: 2 (over y_lo), grp: 16 (over z, y_hi), tp: 8 (over x, core).
Axes of the slice: x: 4, y: 4 (y_hi: 2, y_lo: 2; y = y_hi * 2 + y_lo), z: 8, core: 2. Of those that a mesh axis runs over, the one named last changes fastest.
Arguments:
- hidden_in: bfloat16 [1024, 7168], P(('sec', 'grp', 'tp')), may hold values from -6 to 6
- queries: bfloat16 [1024, 16, 8, 576], P(('sec', 'grp'), None, 'tp'), may hold values from -61 to 61
- latent_cache: bfloat16 [1024, 64, 576], P(('sec', 'grp')), may hold values from -6 to 6
- lengths: int32 [1024], P(('sec', 'grp')), may hold values from 2 to 64, as said below
- w_uv: bfloat16 [16, 8, 512, 128], P(None, 'tp'), may hold values from -0.75 to 0.75
- attn_weight: bfloat16 [16, 8, 128, 7168], P(None, 'tp', None, 'grp'), may hold values from -0.125 to 0.125
- norm_gain: float32 [7168], replicated, may hold values from 0.1 to 1.9
- router: bfloat16 [7168, 32], replicated, may hold values from -0.0625 to 0.0625
- routes: int32 [1024, 8], P(('sec', 'grp', 'tp')), may hold values from 0 to 31, all different within a row; in each aligned block of 4 rows (0 to 3, 4 to 7, ...) at most 2 rows name the same one
- live_counts: int32 [256], P(('sec', 'grp', 'tp')), may hold values from 3 to 4, as said below
- expert_in: bfloat16 [32, 7168, 2, 1024], P(('sec', 'grp'), None, None, 'tp'), may hold values from -0.0625 to 0.0625
- expert_out: bfloat16 [32, 1024, 7168], P(('sec', 'grp'), 'tp'), may hold values from -0.5 to 0.5
Outputs:
- layer_out: bfloat16 [1024, 7168], P(('sec', 'grp', 'tp'))
Inputs may be any that keep to these rules, and one draw needn't show every extreme that they name: `lengths`: some request has exactly 64 cached positions and some has 2. `live_counts`: some device has all 4 slots live and some has exactly 3. `routes`: the 8 experts of a token differ. Within the rows of one device (aligned blocks of 4 rows) no expert is named by more than 2 rows, a bound that some block reaches.
All inputs are finite; a program needn't handle non-finite values.
Results may differ from a plain program's by a relative error of at most 0.018.
Values may be sent and summed in bfloat16 or wider, within the bound.
No kernel may reach another device: no remote copies, remote signals or barrier semaphores. Data moves between devices by JAX's collectives and lax.ppermute only.
A program may use at most 64 MiB of HBM per device.

v0:
```python
import jax
import jax.numpy as jnp
from jax import lax
from jax.sharding import Mesh
from jax.sharding import PartitionSpec as P


GRP = ("grp_0", "grp_1")
SEC_GRP = ("sec", "grp_0", "grp_1")
TP = ("x", "core")
GRP_TP = ("grp_0", "grp_1", "x", "core")
TP_SEC_GRP = ("x", "core", "sec", "grp_0", "grp_1")
SEC_GRP_TP = ("sec", "grp_0", "grp_1", "x", "core")


score_scale = 192.0 ** (-0.5)
route_scale = 2.5


def shifted(x, axis, step):
    size = lax.axis_size(axis)
    return lax.ppermute(x, axis, [(i, (i + step) % size) for i in range(size)])


def rolled(blocks, count):
    size = blocks.shape[0]
    return lax.dynamic_slice_in_dim(jnp.concatenate([blocks, blocks]), size - count, size, 0)


def around_the_ring(block):
    middle = block.shape[0] // 2
    before = {step: shifted(block, "grp_0", step) for step in (1, 2)}
    after = {step: shifted(block, "grp_0", -step) for step in (1, 2)}
    before[3] = shifted(before[2], "grp_0", 1)
    after[3] = shifted(after[2], "grp_0", -1)
    far = jnp.concatenate(
        [shifted(before[2][:middle], "grp_0", 2), shifted(after[2][middle:], "grp_0", -2)]
    )
    near = [block, after[1], after[2], before[2], before[1]]
    return near, [after[3], far, before[3]]


def projected(head_rows, out_block):
    rows, columns = head_rows.shape[0], out_block.shape[1]
    partner = shifted(head_rows, "grp_1", 1)
    products = []
    for gathered in zip(around_the_ring(head_rows), around_the_ring(partner)):
        product = jnp.dot(
            jnp.concatenate(gathered[0] + gathered[1]), out_block, preferred_element_type=jnp.float32
        ).astype(jnp.bfloat16)
        products.append(product.reshape(2, len(gathered[0]), rows, columns))
    near, far = products
    places = jnp.concatenate([near[:, :3], far, near[:, 3:]], axis=1)
    places = rolled(places, lax.axis_index("grp_1"))
    return rolled(jnp.moveaxis(places, 1, 0), lax.axis_index("grp_0"))


def rolled(blocks, count):
    size = blocks.shape[0]
    return lax.dynamic_slice_in_dim(jnp.concatenate([blocks, blocks]), size - count, size, 0)


def own_and_other(array, core, dim):
    size = array.shape[dim] // 2
    return [lax.dynamic_slice_in_dim(array, number * size, size, dim) for number in (core, 1 - core)]


def around_the_ring(block):
    middle = block.shape[0] // 2
    before = {step: shifted(block, "grp_0", step) for step in (2, 1)}
    after = {step: shifted(block, "grp_0", -step) for step in (2, 1)}
    before[3] = shifted(before[2], "grp_0", 1)
    after[3] = shifted(after[2], "grp_0", -1)
    opposite = jnp.concatenate(
        [shifted(before[2][:middle], "grp_0", 2), shifted(after[2][middle:], "grp_0", -2)]
    )
    return [block, after[1], after[2], before[2], before[1]], [after[3], opposite, before[3]]


def projected(head_rows, out_block):
    rows, columns = head_rows.shape[0], out_block.shape[1]
    partner = shifted(head_rows, "grp_1", 1)
    products = []
    for gathered in around_the_ring(jnp.concatenate([head_rows, partner])):
        product = jnp.dot(
            jnp.concatenate(gathered), out_block, preferred_element_type=jnp.float32
        ).astype(jnp.bfloat16)
        products.append(product.reshape(len(gathered), 2, rows, columns))
    near, far = products
    places = jnp.concatenate([near[:3], far, near[3:]])
    places = rolled(jnp.moveaxis(places, 1, 0), lax.axis_index("grp_1"))
    return rolled(jnp.moveaxis(places, 0, 1), lax.axis_index("grp_0"))


def attention_rows(queries, latent_cache, lengths, w_uv):
    latent_width = w_uv.shape[2]
    query_block = queries[:, :, 0, :]
    scores = (
        jnp.einsum("bhr,bpr->bhp", query_block, latent_cache, preferred_element_type=jnp.float32)
        * score_scale
    )
    positions = jnp.arange(latent_cache.shape[1])
    visible = positions[None, None, :] < lengths[:, None, None]
    scores = jnp.where(visible, scores, -1e30)
    highest = jnp.max(scores, axis=2, keepdims=True)
    raised = jnp.exp(scores - highest)
    softmax_weights = (raised / jnp.sum(raised, axis=2, keepdims=True)).astype(jnp.bfloat16)
    latent_out = jnp.einsum(
        "bhp,bpc->bhc",
        softmax_weights,
        latent_cache[:, :, :latent_width],
        preferred_element_type=jnp.float32,
    ).astype(jnp.bfloat16)
    head_out = jnp.einsum(
        "bhc,hcv->bhv", latent_out, w_uv[:, 0], preferred_element_type=jnp.float32
    ).astype(jnp.bfloat16)
    return head_out.reshape(head_out.shape[0], -1)


def layer(
    hidden_in,
    queries,
    latent_cache,
    lengths,
    w_uv,
    attn_weight,
    norm_gain,
    router,
    routes,
    live_counts,
    expert_in,
    expert_out,
):
    count_of_tokens, width = hidden_in.shape
    groups = lax.axis_size(GRP)
    slices = lax.axis_size(TP)
    chips = lax.axis_size("x")
    chip, core = lax.axis_index("x"), lax.axis_index("core")
    part = width // slices
    slice_width = expert_in.shape[3]

    head_rows = attention_rows(queries, latent_cache, lengths, w_uv)
    head_rows, expert_in, expert_out = lax.optimization_barrier(
        (head_rows, expert_in, expert_out)
    )

    rows_of_chip = width // chips
    in_parts = [
        lax.dynamic_slice_in_dim(expert_in[0], (chip - step) % chips * rows_of_chip, rows_of_chip, 0)
        for step in range(chips)
    ]
    in_parts[1:] = [shifted(in_parts[step], "x", -step) for step in range(1, chips)]
    out_before, out_after = shifted(expert_out[0], "x", 1), shifted(expert_out[0], "x", -1)

    out_block = attn_weight[:, 0].reshape(-1, attn_weight.shape[3])
    partial_value = projected(head_rows, out_block)
    partial_value = partial_value.reshape(groups * slices, count_of_tokens, -1)
    arrived = lax.all_to_all(partial_value, GRP_TP, split_axis=0, concat_axis=0, tiled=True)
    summed = arrived.reshape(groups, slices, count_of_tokens, -1).astype(jnp.float32).sum(axis=1)
    attention = jnp.moveaxis(summed.astype(jnp.bfloat16), 0, 1).reshape(count_of_tokens, width)

    residual = hidden_in.astype(jnp.float32) + attention.astype(jnp.float32)
    normalized_input = (
        residual
        * lax.rsqrt(jnp.mean(residual * residual, axis=1, keepdims=True) + 1e-06)
        * norm_gain
    ).astype(jnp.bfloat16)
    experts = router.shape[1]
    per_token = routes.shape[1]
    capacity = max(2, 2 * count_of_tokens * per_token // experts)
    affinity = jax.nn.sigmoid(jnp.dot(normalized_input, router, preferred_element_type=jnp.float32))
    picked = routes[:, :, None] == jnp.arange(experts)[None, None, :]
    chosen = jnp.sum(jnp.where(picked, affinity[:, None, :], 0.0), axis=2)
    living = jnp.arange(count_of_tokens) < live_counts[0]
    gate_weights = (
        route_scale
        * chosen
        / jnp.sum(chosen, axis=1, keepdims=True)
        * living[:, None].astype(jnp.float32)
    )
    routed = jnp.any(picked, axis=1) & living[:, None]
    routed_count = routed.astype(jnp.int32)
    slot_index = jnp.cumsum(routed_count, axis=0) - routed_count
    placed_tokens = routed[:, :, None] & (
        slot_index[:, :, None] == jnp.arange(capacity)[None, None, :]
    )
    expert_gate = jnp.sum(jnp.where(picked, gate_weights[:, :, None], 0.0), axis=1)
    outgoing = jnp.einsum(
        "poy,ptj->toyj",
        placed_tokens.astype(jnp.bfloat16),
        normalized_input.reshape(count_of_tokens, slices, part),
        preferred_element_type=jnp.float32,
    ).astype(jnp.bfloat16)
    combine_rows = placed_tokens.astype(jnp.float32) * expert_gate[:, :, None]
    outgoing = outgoing.reshape(slices * experts, capacity, part)
    rows = lax.all_to_all(
        outgoing, TP_SEC_GRP, split_axis=0, concat_axis=0, tiled=True
    ).reshape(-1, part)

    in_parts, out_before, out_after, _ = lax.optimization_barrier(
        (in_parts, out_before, out_after, outgoing)
    )
    in_columns = jnp.concatenate(
        [p.reshape(rows_of_chip, 2 * slice_width) for p in in_parts], axis=1
    )
    in_own, in_other = own_and_other(in_columns, core, 0)
    middle = slice_width // 2
    out_opposite = [
        shifted(out_before[:middle], "x", 1), shifted(out_after[middle:], "x", -1)
    ]
    out_own = jnp.concatenate([expert_out[0], out_after, *out_opposite, out_before])
    out_other = shifted(out_own, "core", 1)

    other_rows = shifted(rows, "core", 1)
    products = jnp.dot(rows, in_own, preferred_element_type=jnp.float32) + jnp.dot(
        other_rows, in_other, preferred_element_type=jnp.float32
    )
    gate_up = lax.all_to_all(
        products.astype(jnp.bfloat16).reshape(chips, -1, products.shape[1]),
        "x", split_axis=0, concat_axis=0, tiled=True,
    )
    parts_of = gate_up.astype(jnp.float32)
    activated = []
    for number in range(chips):
        starts = [(number - p) % chips * 2 * slice_width for p in range(chips)]
        gate_value, up_value = (
            sum(
                parts_of[p, :, start + first : start + first + slice_width]
                for p, start in enumerate(starts)
            )
            for first in (0, slice_width)
        )
        activated.append((jax.nn.silu(gate_value) * up_value).astype(jnp.bfloat16))
    activated = jnp.concatenate(list(rolled(jnp.stack(activated), chips - chip)), axis=1)
    hidden_own, hidden_sent = own_and_other(activated, core, 0)
    hidden_other = shifted(hidden_sent, "core", 1)
    values = (
        jnp.dot(hidden_own, out_own, preferred_element_type=jnp.float32)
        + jnp.dot(hidden_other, out_other, preferred_element_type=jnp.float32)
    ).astype(jnp.bfloat16)
    back = lax.all_to_all(
        values.reshape(experts, capacity, width), SEC_GRP, split_axis=0, concat_axis=0, tiled=True
    ).reshape(experts * capacity, width)
    coarse = lax.reduce_precision(combine_rows, 8, 7)
    weights = jnp.concatenate([coarse, combine_rows - coarse], axis=0).astype(jnp.bfloat16)
    mixed = jnp.dot(
        weights.reshape(2 * count_of_tokens, -1), back, preferred_element_type=jnp.float32
    )
    expert_mix = mixed[:count_of_tokens] + mixed[count_of_tokens:]
    return (residual + expert_mix).astype(jnp.bfloat16)


def solution(mesh):
    torus = Mesh(
        mesh.devices.reshape(mesh.shape["sec"], 8, 2, mesh.shape["tp"] // 2, 2), SEC_GRP_TP
    )
    in_specs = (
        P(SEC_GRP_TP, None),
        P(SEC_GRP, None, TP, None),
        P(SEC_GRP, None, None),
        P(SEC_GRP),
        P(None, TP, None, None),
        P(None, TP, None, GRP),
        P(),
        P(),
        P(SEC_GRP_TP, None),
        P(SEC_GRP_TP),
        P(SEC_GRP, None, None, TP),
        P(SEC_GRP, TP, None),
    )
    out_specs = P(SEC_GRP_TP, None)
    return jax.shard_map(layer, mesh=torus, in_specs=in_specs, out_specs=out_specs, check_vma=False)
```

profile of v0, /device:TPU:8, one launch (start us, length us, event | category | flops | bytes accessed | tf_op | source)
XLA Modules:
  0.0 274.0 jit_solution(196497962990556977)
XLA Ops:
  0.9 2.9 %fusion.30 = f32[32,16,64]{2,1,0:T(8,128)S(1)} fusion(bf16[32,64,576]{2,1,0:T(8,128)(2,1)} %param.14, bf16[32,16,1,576]{3,1,2,0:T(8,128)(2,1)} %param.13, pred[32,64]{1,0:T(8,128)(4,1)S(1)} %iota_compare_fusion.1), kind=kOutput, calls=%fused_computation.27 | convolution fusion | flops 37814272 | bytes 3082240 | tf_op jit(solution)/shard_map/bhr,bpr->bhp/dot_general | solution.py:99
  4.0 2.5 fusion.19
  7.2 2.4 collective-permute-start
  10.3 3.8 %collective-permute-done = bf16[32,2048]{1,0:T(8,128)(2,1)S(1)} collective-permute-done((bf16[32,2048]{1,0:T(8,128)(2,1)S(1)}, bf16[32,2048]{1,0:T(8,128)(2,1)S(1)}, u32[]{:S(2)}, u32[]{:S(2)}) %collective-permute-start) | collective-permute-done | bytes 131104 | tf_op jit(solution)/shard_map/ppermute | solution.py:22
  14.7 6.3 %collective-permute-start.2 = (bf16[64,2048]{1,0:T(8,128)(2,1)S(1)}, bf16[64,2048]{1,0:T(8,128)(2,1)S(1)}, u32[]{:S(2)}, u32[]{:S(2)}) collective-permute-start(bf16[64,2048]{1,0:T(8,128)(2,1)S(1)} %get-tuple-element.45), channel_id=1, source_target_pairs={{0,96},{16,112},{32,0},{48,16},{64,32},{80,48},{96,64},{112,80},{1... | collective-permute-start | bytes 786440 | tf_op jit(solution)/shard_map/ppermute | solution.py:22
  21.0 3.7 %collective-permute-start.1 = (bf16[64,2048]{1,0:T(8,128)(2,1)S(1)}, bf16[64,2048]{1,0:T(8,128)(2,1)S(1)}, u32[]{:S(2)}, u32[]{:S(2)}) collective-permute-start(bf16[64,2048]{1,0:T(8,128)(2,1)S(1)} %get-tuple-element.45), channel_id=1, source_target_pairs={{0,112},{16,0},{32,16},{48,32},{64,48},{80,64},{96,80},{112,96},{1... | collective-permute-start | bytes 786440 | tf_op jit(solution)/shard_map/ppermute | solution.py:22
  24.7 1.5 collective-permute-start.12
  26.2 4.0 %copy.37 = bf16[16,1,128,448]{2,0,3,1:T(8,128)(2,1)} copy(bf16[16,1,128,448]{2,3,1,0:T(8,128)(2,1)} %param.17) | data formatting | bytes 3670016 | tf_op args[5]
  30.2 2.3 collective-permute-done.2
  32.5 4.8 %collective-permute-start.7 = (bf16[32,2048]{1,0:T(8,128)(2,1)S(1)}, bf16[32,2048]{1,0:T(8,128)(2,1)S(1)}, u32[]{:S(2)}, u32[]{:S(2)}) collective-permute-start(bf16[32,2048]{1,0:T(8,128)(2,1)S(1)} %slice.174), channel_id=1, source_target_pairs={{0,96},{16,112},{32,0},{48,16},{64,32},{80,48},{96,64},{112,80},{1... | collective-permute-start | bytes 393224 | tf_op jit(solution)/shard_map/ppermute | solution.py:22
  37.4 3.5 %collective-permute-done.1 = bf16[64,2048]{1,0:T(8,128)(2,1)S(1)} collective-permute-done((bf16[64,2048]{1,0:T(8,128)(2,1)S(1)}, bf16[64,2048]{1,0:T(8,128)(2,1)S(1)}, u32[]{:S(2)}, u32[]{:S(2)}) %collective-permute-start.1) | collective-permute-done | bytes 262176 | tf_op jit(solution)/shard_map/ppermute | solution.py:22
  43.1 3.2 %collective-permute-start.5 = (bf16[64,2048]{1,0:T(8,128)(2,1)S(1)}, bf16[64,2048]{1,0:T(8,128)(2,1)S(1)}, u32[]{:S(2)}, u32[]{:S(2)}) collective-permute-start(bf16[64,2048]{1,0:T(8,128)(2,1)S(1)} %collective-permute-done.2), channel_id=1, source_target_pairs={{0,112},{16,0},{32,16},{48,32},{64,48},{80,64},{96,80},{112,96},{1... | collective-permute-start | bytes 786440 | tf_op jit(solution)/shard_map/ppermute | solution.py:22
  47.0 2.2 fusion.22
  49.3 3.0 %collective-permute-start.13 = (bf16[128,7168]{1,0:T(8,128)(2,1)}, bf16[128,7168]{1,0:T(8,128)(2,1)}, u32[]{:S(2)}, u32[]{:S(2)}) collective-permute-start(bf16[128,7168]{1,0:T(8,128)(2,1)} %bitcast.21), channel_id=1, source_target_pairs={{0,6},{2,0},{4,2},{6,4},{1,7},{3,1},{5,3},{7,5},{8,14},{10,8},{12,... | collective-permute-start | bytes 5505032 | tf_op jit(solution)/shard_map/ppermute | solution.py:22
  54.5 9.2 %all-to-all-start = ((bf16[128,4,448]{2,1,0:T(4,128)(2,1)}), bf16[128,4,448]{2,1,0:T(4,128)(2,1)S(1)}, u32[]{:S(2)}, u32[]{:S(2)}) async-start(bf16[128,4,448]{2,1,0:T(4,128)(2,1)} %reshape.187), calls=%async_computation | async-start | bytes 1048576 | tf_op jit(solution)/shard_map/all_to_all | solution.py:158
  63.8 5.0 %dynamic-slice_bitcast_fusion = (bf16[1792,2,128]{2,1,0:T(2,128)(2,1)}, bf16[1792,2,128]{2,1,0:T(2,128)(2,1)}, bf16[1792,2,128]{2,1,0:T(2,128)(2,1)}, bf16[1792,2,128]{2,1,0:T(2,128)(2,1)S(1)}) fusion(bf16[1,7168,2,128]{3,2,1,0:T(2,128)(2,1)} %param.22, s32[]{:T(128)S(6)} %select_n.76, s32[]{:T(128)S(6)} %select_n.74, s32[]{:T(128)S(6)} %select_n.72, ...), kind=kLoop, calls=%fused_computation.43 | loop fusion | bytes 7340048 | tf_op jit(solution)/shard_map/dynamic_slice | solution.py:149
  68.7 2.3 collective-permute-start.9
  73.7 26.2 %all-to-all-done = bf16[128,4,448]{2,1,0:T(4,128)(2,1)S(1)} async-done(((bf16[128,4,448]{2,1,0:T(4,128)(2,1)}), bf16[128,4,448]{2,1,0:T(4,128)(2,1)S(1)}, u32[]{:S(2)}, u32[]{:S(2)}) %all-to-all-start) | async-done | bytes 458784 | tf_op jit(solution)/shard_map/all_to_all | solution.py:158
  100.3 1.0 multiply_reduce_fusion
  102.3 1.2 fusion.39
  104.5 28.4 %collective-permute-done.9 = bf16[1792,2,128]{2,1,0:T(2,128)(2,1)} collective-permute-done((bf16[1792,2,128]{2,1,0:T(2,128)(2,1)}, bf16[1792,2,128]{2,1,0:T(2,128)(2,1)}, u32[]{:S(2)}, u32[]{:S(2)}) %collective-permute-start.9) | collective-permute-done | bytes 917536 | tf_op jit(solution)/shard_map/ppermute | solution.py:22
  132.9 2.2 collective-permute-start.15
  135.1 2.9 %constant_dynamic-update-slice_fusion.20 = bf16[512,7168]{1,0:T(8,128)(2,1)} fusion(bf16[1,128,7168]{2,1,0:T(8,128)(2,1)} %param.23), kind=kLoop, calls=%fused_computation.125 | loop fusion | bytes 3670016
  138.0 1.2 slice.169
  139.2 1.7 collective-permute-start.16
  140.9 2.8 %constant_dynamic-update-slice_fusion.19 = bf16[512,7168]{1,0:T(8,128)(2,1)} fusion(bf16[512,7168]{1,0:T(8,128)(2,1)} %constant_dynamic-update-slice_fusion.20, bf16[128,7168]{1,0:T(8,128)(2,1)} %collective-permute-done.13), kind=kLoop, calls=%fused_computation.124 | loop fusion | bytes 3670016
  143.8 7.0 %collective-permute-done.15 = bf16[64,7168]{1,0:T(8,128)(2,1)S(1)} collective-permute-done((bf16[64,7168]{1,0:T(8,128)(2,1)S(1)}, bf16[64,7168]{1,0:T(8,128)(2,1)S(1)}, u32[]{:S(2)}, u32[]{:S(2)}) %collective-permute-start.15) | collective-permute-done | bytes 917536 | tf_op jit(solution)/shard_map/ppermute | solution.py:22
  150.8 1.0 constant_dynamic-update-slice_fusion.18
  151.8 4.5 %collective-permute-done.16 = bf16[64,7168]{1,0:T(8,128)(2,1)S(1)} collective-permute-done((bf16[64,7168]{1,0:T(8,128)(2,1)S(1)}, bf16[64,7168]{1,0:T(8,128)(2,1)S(1)}, u32[]{:S(2)}, u32[]{:S(2)}) %collective-permute-start.16) | collective-permute-done | bytes 917536 | tf_op jit(solution)/shard_map/ppermute | solution.py:22
  156.2 1.0 constant_dynamic-update-slice_fusion.17
  157.2 1.4 constant_dynamic-update-slice_fusion.16
  158.6 1.9 copy.41
  160.5 10.3 %all-to-all-start.1 = ((bf16[256,2,896]{2,1,0:T(2,128)(2,1)}), bf16[256,2,896]{2,1,0:T(2,128)(2,1)S(1)}, u32[]{:S(2)}, u32[]{:S(2)}) async-start(bf16[256,2,896]{2,1,0:T(2,128)(2,1)} %copy.41), calls=%async_computation.1 | async-start | bytes 1835008 | tf_op jit(solution)/shard_map/all_to_all | solution.py:196
  170.8 1.1 bitcast_dynamic-update-slice_fusion.3
  171.9 2.3 bitcast_dynamic-update-slice_fusion.2
  174.2 25.7 %all-to-all-done.1 = bf16[256,2,896]{2,1,0:T(2,128)(2,1)S(1)} async-done(((bf16[256,2,896]{2,1,0:T(2,128)(2,1)}), bf16[256,2,896]{2,1,0:T(2,128)(2,1)S(1)}, u32[]{:S(2)}, u32[]{:S(2)}) %all-to-all-start.1) | async-done | bytes 917536 | tf_op jit(solution)/shard_map/all_to_all | solution.py:196
  200.3 2.3 bitcast_dynamic-update-slice_fusion.1
  202.6 2.3 bitcast_dynamic-update-slice_fusion
  204.9 2.7 %fusion.12 = f32[512,1024]{1,0:T(8,128)S(1)} fusion(bf16[512,896]{1,0:T(8,128)(2,1)S(1)} %reshape.191, bf16[1792,1024]{1,0:T(8,128)(2,1)} %bitcast_dynamic-update-slice_fusion, s32[]{:T(128)S(6)} %select_n.77), kind=kOutput, calls=%fused_computation.15 | convolution fusion | flops 939524096 | bytes 4849668 | tf_op jit(solution)/shard_map/dot_general | solution.py:215
  207.6 3.8 %add_convert_fusion = bf16[512,1024]{1,0:T(8,128)(2,1)} fusion(f32[512,1024]{1,0:T(8,128)S(1)} %fusion.12, bf16[512,896]{1,0:T(8,128)(2,1)S(1)} %collective-permute-done.14, bf16[1792,1024]{1,0:T(8,128)(2,1)} %bitcast_dynamic-update-slice_fusion, s32[]{:T(128)S(6)} %select_n.78), kind=kOutput, calls=%fused_computation.6 | convolution fusion | flops 940572672 | bytes 5898244 | tf_op jit(solution)/shard_map/dot_general | solution.py:215
  211.4 3.5 %all-to-all-start.2 = ((bf16[4,128,1024]{2,1,0:T(8,128)(2,1)}), bf16[4,128,1024]{2,1,0:T(8,128)(2,1)S(1)}, u32[]{:S(2)}, u32[]{:S(2)}) async-start(bf16[4,128,1024]{2,1,0:T(8,128)(2,1)} %bitcast.22), calls=%async_computation.2 | async-start | bytes 2097152 | tf_op jit(solution)/shard_map/all_to_all | solution.py:218
  214.9 16.0 %all-to-all-done.2 = bf16[4,128,1024]{2,1,0:T(8,128)(2,1)S(1)} async-done(((bf16[4,128,1024]{2,1,0:T(8,128)(2,1)}), bf16[4,128,1024]{2,1,0:T(8,128)(2,1)S(1)}, u32[]{:S(2)}, u32[]{:S(2)}) %all-to-all-start.2) | async-done | bytes 1048608 | tf_op jit(solution)/shard_map/all_to_all | solution.py:218
  231.6 1.2 collective-permute-done.17
  232.9 4.5 %fusion.86 = f32[64,7168]{1,0:T(8,128)S(1)} fusion(bf16[64,512]{1,0:T(8,128)(2,1)S(1)} %collective-permute-done.17, bf16[512,7168]{1,0:T(8,128)(2,1)} %collective-permute-done.18), kind=kOutput, calls=%fused_computation.160 | convolution fusion | flops 469762048 | bytes 9240576 | tf_op jit(solution)/shard_map/dot_general | solution.py:239
  237.4 4.5 %fusion.1 = bf16[64,7168]{1,0:T(8,128)(2,1)S(1)} fusion(f32[64,7168]{1,0:T(8,128)S(1)} %fusion.86, bf16[512,7168]{1,0:T(8,128)(2,1)} %constant_dynamic-update-slice_fusion.16, bf16[128,512]{1,0:T(8,128)(2,1)S(1)} %pad_maximum_fusion, s32[]{:T(128)S(6)} %select_n.80), kind=kOutput, calls=%fused_computation.2 | convolution fusion | flops 470679552 | bytes 10158084 | tf_op jit(solution)/shard_map/dot_general | solution.py:238
  241.9 1.3 reshape.197
  243.1 5.1 %all-to-all-start.3 = ((bf16[32,2,7168]{2,1,0:T(2,128)(2,1)}), bf16[32,2,7168]{2,1,0:T(2,128)(2,1)S(1)}, u32[]{:S(2)}, u32[]{:S(2)}) async-start(bf16[32,2,7168]{2,1,0:T(2,128)(2,1)} %reshape.197), calls=%async_computation.3 | async-start | bytes 1835008 | tf_op jit(solution)/shard_map/all_to_all | solution.py:241
  248.2 24.8 %all-to-all-done.3 = bf16[32,2,7168]{2,1,0:T(2,128)(2,1)S(1)} async-done(((bf16[32,2,7168]{2,1,0:T(2,128)(2,1)}), bf16[32,2,7168]{2,1,0:T(2,128)(2,1)S(1)}, u32[]{:S(2)}, u32[]{:S(2)}) %all-to-all-start.3) | async-done | bytes 917536 | tf_op jit(solution)/shard_map/all_to_all | solution.py:241
  (84 shorter events, 14.7 us)
Async XLA Ops:
  0.0 6.5 %copy-start = (bf16[16,1,512,128]{3,2,1,0:T(8,128)(2,1)S(1)}, bf16[16,1,512,128]{3,2,1,0:T(8,128)(2,1)}, u32[]{:S(2)}) copy-start(bf16[16,1,512,128]{3,2,1,0:T(8,128)(2,1)} %param.16) | copy-start | bytes 6291460
  7.2 6.8 %collective-permute-start = (bf16[32,2048]{1,0:T(8,128)(2,1)S(1)}, bf16[32,2048]{1,0:T(8,128)(2,1)S(1)}, u32[]{:S(2)}, u32[]{:S(2)}) collective-permute-start(bf16[32,2048]{1,0:T(8,128)(2,1)S(1)} %bitcast.105), channel_id=1, source_target_pairs={{0,8},{8,0},{1,9},{9,1},{2,10},{10,2},{3,11},{11,3},{4,12},{12,4},... | collective-permute-start | bytes 393224 | tf_op jit(solution)/shard_map/ppermute | solution.py:22
  14.7 17.8 %collective-permute-start.2 = (bf16[64,2048]{1,0:T(8,128)(2,1)S(1)}, bf16[64,2048]{1,0:T(8,128)(2,1)S(1)}, u32[]{:S(2)}, u32[]{:S(2)}) collective-permute-start(bf16[64,2048]{1,0:T(8,128)(2,1)S(1)} %get-tuple-element.45), channel_id=1, source_target_pairs={{0,96},{16,112},{32,0},{48,16},{64,32},{80,48},{96,64},{112,80},{1... | collective-permute-start | bytes 786440 | tf_op jit(solution)/shard_map/ppermute | solution.py:22
  21.0 16.3 %collective-permute-start.3 = (bf16[64,2048]{1,0:T(8,128)(2,1)S(1)}, bf16[64,2048]{1,0:T(8,128)(2,1)S(1)}, u32[]{:S(2)}, u32[]{:S(2)}) collective-permute-start(bf16[64,2048]{1,0:T(8,128)(2,1)S(1)} %get-tuple-element.45), channel_id=1, source_target_pairs={{0,32},{16,48},{32,64},{48,80},{64,96},{80,112},{96,0},{112,16},{1... | collective-permute-start | bytes 786440 | tf_op jit(solution)/shard_map/ppermute | solution.py:22
  21.0 19.9 %collective-permute-start.1 = (bf16[64,2048]{1,0:T(8,128)(2,1)S(1)}, bf16[64,2048]{1,0:T(8,128)(2,1)S(1)}, u32[]{:S(2)}, u32[]{:S(2)}) collective-permute-start(bf16[64,2048]{1,0:T(8,128)(2,1)S(1)} %get-tuple-element.45), channel_id=1, source_target_pairs={{0,112},{16,0},{32,16},{48,32},{64,48},{80,64},{96,80},{112,96},{1... | collective-permute-start | bytes 786440 | tf_op jit(solution)/shard_map/ppermute | solution.py:22
  24.7 108.1 %collective-permute-start.12 = (bf16[128,7168]{1,0:T(8,128)(2,1)}, bf16[128,7168]{1,0:T(8,128)(2,1)S(1)}, u32[]{:S(2)}, u32[]{:S(2)}) collective-permute-start(bf16[128,7168]{1,0:T(8,128)(2,1)} %bitcast.21), channel_id=1, source_target_pairs={{0,2},{2,4},{4,6},{6,0},{1,3},{3,5},{5,7},{7,1},{8,10},{10,12},{12... | collective-permute-start | bytes 5505032 | tf_op jit(solution)/shard_map/ppermute | solution.py:22
  30.1 16.9 %copy-start.2 = (bf16[16,1,128,448]{2,0,3,1:T(8,128)(2,1)S(1)}, bf16[16,1,128,448]{2,0,3,1:T(8,128)(2,1)}, u32[]{:S(2)}) copy-start(bf16[16,1,128,448]{2,0,3,1:T(8,128)(2,1)} %copy.37) | copy-start | bytes 5505028
  30.1 12.9 %collective-permute-start.4 = (bf16[64,2048]{1,0:T(8,128)(2,1)S(1)}, bf16[64,2048]{1,0:T(8,128)(2,1)S(1)}, u32[]{:S(2)}, u32[]{:S(2)}) collective-permute-start(bf16[64,2048]{1,0:T(8,128)(2,1)S(1)} %get-tuple-element.45), channel_id=1, source_target_pairs={{0,16},{16,32},{32,48},{48,64},{64,80},{80,96},{96,112},{112,0},{1... | collective-permute-start | bytes 786440 | tf_op jit(solution)/shard_map/ppermute | solution.py:22
  32.5 16.8 %collective-permute-start.7 = (bf16[32,2048]{1,0:T(8,128)(2,1)S(1)}, bf16[32,2048]{1,0:T(8,128)(2,1)S(1)}, u32[]{:S(2)}, u32[]{:S(2)}) collective-permute-start(bf16[32,2048]{1,0:T(8,128)(2,1)S(1)} %slice.174), channel_id=1, source_target_pairs={{0,96},{16,112},{32,0},{48,16},{64,32},{80,48},{96,64},{112,80},{1... | collective-permute-start | bytes 393224 | tf_op jit(solution)/shard_map/ppermute | solution.py:22
  37.3 15.0 %collective-permute-start.6 = (bf16[32,2048]{1,0:T(8,128)(2,1)S(1)}, bf16[32,2048]{1,0:T(8,128)(2,1)S(1)}, u32[]{:S(2)}, u32[]{:S(2)}) collective-permute-start(bf16[32,2048]{1,0:T(8,128)(2,1)S(1)} %slice.173), channel_id=1, source_target_pairs={{0,32},{16,48},{32,64},{48,80},{64,96},{80,112},{96,0},{112,16},{1... | collective-permute-start | bytes 393224 | tf_op jit(solution)/shard_map/ppermute | solution.py:22
  40.9 11.4 %collective-permute-start.8 = (bf16[64,2048]{1,0:T(8,128)(2,1)S(1)}, bf16[64,2048]{1,0:T(8,128)(2,1)S(1)}, u32[]{:S(2)}, u32[]{:S(2)}) collective-permute-start(bf16[64,2048]{1,0:T(8,128)(2,1)S(1)} %collective-permute-done.3), channel_id=1, source_target_pairs={{0,16},{16,32},{32,48},{48,64},{64,80},{80,96},{96,112},{112,0},{1... | collective-permute-start | bytes 786440 | tf_op jit(solution)/shard_map/ppermute | solution.py:22
  43.1 9.2 %collective-permute-start.5 = (bf16[64,2048]{1,0:T(8,128)(2,1)S(1)}, bf16[64,2048]{1,0:T(8,128)(2,1)S(1)}, u32[]{:S(2)}, u32[]{:S(2)}) collective-permute-start(bf16[64,2048]{1,0:T(8,128)(2,1)S(1)} %collective-permute-done.2), channel_id=1, source_target_pairs={{0,112},{16,0},{32,16},{48,32},{64,48},{80,64},{96,80},{112,96},{1... | collective-permute-start | bytes 786440 | tf_op jit(solution)/shard_map/ppermute | solution.py:22
  49.3 83.5 %collective-permute-start.13 = (bf16[128,7168]{1,0:T(8,128)(2,1)}, bf16[128,7168]{1,0:T(8,128)(2,1)}, u32[]{:S(2)}, u32[]{:S(2)}) collective-permute-start(bf16[128,7168]{1,0:T(8,128)(2,1)} %bitcast.21), channel_id=1, source_target_pairs={{0,6},{2,0},{4,2},{6,4},{1,7},{3,1},{5,3},{7,5},{8,14},{10,8},{12,... | collective-permute-start | bytes 5505032 | tf_op jit(solution)/shard_map/ppermute | solution.py:22
  54.5 45.4 %all-to-all-start = ((bf16[128,4,448]{2,1,0:T(4,128)(2,1)}), bf16[128,4,448]{2,1,0:T(4,128)(2,1)S(1)}, u32[]{:S(2)}, u32[]{:S(2)}) async-start(bf16[128,4,448]{2,1,0:T(4,128)(2,1)} %reshape.187), calls=%async_computation | async-start | bytes 1048576 | tf_op jit(solution)/shard_map/all_to_all | solution.py:158
  63.8 9.7 %copy-start.4 = (s32[4,8]{1,0:T(4,128)S(1)}, s32[4,8]{1,0:T(4,128)}, u32[]{:S(2)}) copy-start(s32[4,8]{1,0:T(4,128)} %param.20) | copy-start | bytes 388
  68.7 64.1 %collective-permute-start.9 = (bf16[1792,2,128]{2,1,0:T(2,128)(2,1)}, bf16[1792,2,128]{2,1,0:T(2,128)(2,1)}, u32[]{:S(2)}, u32[]{:S(2)}) collective-permute-start(bf16[1792,2,128]{2,1,0:T(2,128)(2,1)} %get-tuple-element.39), channel_id=1, source_target_pairs={{0,6},{2,0},{4,2},{6,4},{1,7},{3,1},{5,3},{7,5},{8,14},{10,8},{12,... | collective-permute-start | bytes 2752520 | tf_op jit(solution)/shard_map/ppermute | solution.py:22
  71.1 61.8 %collective-permute-start.10 = (bf16[1792,2,128]{2,1,0:T(2,128)(2,1)}, bf16[1792,2,128]{2,1,0:T(2,128)(2,1)}, u32[]{:S(2)}, u32[]{:S(2)}) collective-permute-start(bf16[1792,2,128]{2,1,0:T(2,128)(2,1)} %get-tuple-element.38), channel_id=1, source_target_pairs={{0,4},{2,6},{4,0},{6,2},{1,5},{3,7},{5,1},{7,3},{8,12},{10,14},{12... | collective-permute-start | bytes 2752520 | tf_op jit(solution)/shard_map/ppermute | solution.py:22
  71.9 60.9 %collective-permute-start.11 = (bf16[1792,2,128]{2,1,0:T(2,128)(2,1)}, bf16[1792,2,128]{2,1,0:T(2,128)(2,1)}, u32[]{:S(2)}, u32[]{:S(2)}) collective-permute-start(bf16[1792,2,128]{2,1,0:T(2,128)(2,1)} %get-tuple-element.37), channel_id=1, source_target_pairs={{0,2},{2,4},{4,6},{6,0},{1,3},{3,5},{5,7},{7,1},{8,10},{10,12},{12... | collective-permute-start | bytes 2752520 | tf_op jit(solution)/shard_map/ppermute | solution.py:22
  132.9 17.9 %collective-permute-start.15 = (bf16[64,7168]{1,0:T(8,128)(2,1)S(1)}, bf16[64,7168]{1,0:T(8,128)(2,1)S(1)}, u32[]{:S(2)}, u32[]{:S(2)}) collective-permute-start(bf16[64,7168]{1,0:T(8,128)(2,1)S(1)} %slice.168), channel_id=1, source_target_pairs={{0,2},{2,4},{4,6},{6,0},{1,3},{3,5},{5,7},{7,1},{8,10},{10,12},{12... | collective-permute-start | bytes 2752520 | tf_op jit(solution)/shard_map/ppermute | solution.py:22
  139.2 17.0 %collective-permute-start.16 = (bf16[64,7168]{1,0:T(8,128)(2,1)S(1)}, bf16[64,7168]{1,0:T(8,128)(2,1)S(1)}, u32[]{:S(2)}, u32[]{:S(2)}) collective-permute-start(bf16[64,7168]{1,0:T(8,128)(2,1)S(1)} %slice.169), channel_id=1, source_target_pairs={{0,6},{2,0},{4,2},{6,4},{1,7},{3,1},{5,3},{7,5},{8,14},{10,8},{12,... | collective-permute-start | bytes 2752520 | tf_op jit(solution)/shard_map/ppermute | solution.py:22
  158.6 74.3 %collective-permute-start.18 = (bf16[512,7168]{1,0:T(8,128)(2,1)}, bf16[512,7168]{1,0:T(8,128)(2,1)}, u32[]{:S(2)}, u32[]{:S(2)}) collective-permute-start(bf16[512,7168]{1,0:T(8,128)(2,1)} %constant_dynamic-update-slice_fusion.16), channel_id=1, source_target_pairs={{0,1},{1,0},{2,3},{3,2},{4,5},{5,4},{6,7},{7,6},{8,9},{9,8},{10,11... | collective-permute-start | bytes 22020104 | tf_op jit(solution)/shard_map/ppermute | solution.py:22
  160.5 39.4 %all-to-all-start.1 = ((bf16[256,2,896]{2,1,0:T(2,128)(2,1)}), bf16[256,2,896]{2,1,0:T(2,128)(2,1)S(1)}, u32[]{:S(2)}, u32[]{:S(2)}) async-start(bf16[256,2,896]{2,1,0:T(2,128)(2,1)} %copy.41), calls=%async_computation.1 | async-start | bytes 1835008 | tf_op jit(solution)/shard_map/all_to_all | solution.py:196
  200.2 7.4 %collective-permute-start.14 = (bf16[512,896]{1,0:T(8,128)(2,1)S(1)}, bf16[512,896]{1,0:T(8,128)(2,1)S(1)}, u32[]{:S(2)}, u32[]{:S(2)}) collective-permute-start(bf16[512,896]{1,0:T(8,128)(2,1)S(1)} %reshape.191), channel_id=1, source_target_pairs={{0,1},{1,0},{2,3},{3,2},{4,5},{5,4},{6,7},{7,6},{8,9},{9,8},{10,11... | collective-permute-start | bytes 2752520 | tf_op jit(solution)/shard_map/ppermute | solution.py:22
  211.4 19.5 %all-to-all-start.2 = ((bf16[4,128,1024]{2,1,0:T(8,128)(2,1)}), bf16[4,128,1024]{2,1,0:T(8,128)(2,1)S(1)}, u32[]{:S(2)}, u32[]{:S(2)}) async-start(bf16[4,128,1024]{2,1,0:T(8,128)(2,1)} %bitcast.22), calls=%async_computation.2 | async-start | bytes 2097152 | tf_op jit(solution)/shard_map/all_to_all | solution.py:218
  231.5 1.3 collective-permute-start.17
  241.8 31.5 %copy-start.3 = (bf16[4,7168]{1,0:T(4,128)(2,1)S(1)}, bf16[4,7168]{1,0:T(4,128)(2,1)}, u32[]{:S(2)}) copy-start(bf16[4,7168]{1,0:T(4,128)(2,1)} %param.12) | copy-start | bytes 172036
  241.9 32.2 %copy-start.1 = (bf16[16,1,512,128]{3,2,1,0:T(8,128)(2,1)S(1)}, bf16[16,1,512,128]{3,2,1,0:T(8,128)(2,1)}, u32[]{:S(2)}) copy-start(bf16[16,1,512,128]{3,2,1,0:T(8,128)(2,1)} %param.16) | copy-start | bytes 6291460
  243.1 29.9 %all-to-all-start.3 = ((bf16[32,2,7168]{2,1,0:T(2,128)(2,1)}), bf16[32,2,7168]{2,1,0:T(2,128)(2,1)S(1)}, u32[]{:S(2)}, u32[]{:S(2)}) async-start(bf16[32,2,7168]{2,1,0:T(2,128)(2,1)} %reshape.197), calls=%async_computation.3 | async-start | bytes 1835008 | tf_op jit(solution)/shard_map/all_to_all | solution.py:241
where the time goes:
time: 276 us; the launch traced here: 274 us
  waiting for transfers between devices  143 us (52%)
  starting transfers between devices  61.2 us (22%)
  local copies, waits for them, and re-layouts  36.4 us (13%)
  matrix products  26.3 us (10%)
  other arithmetic  5.58 us (2%)
    ppermute x19, waiting for transfers between devices, shifted(): return lax.ppermute(x, axis, [(i, (i + step) % size) for i in range(size)])  50.7 us
    ppermute x19, starting transfers between devices, shifted(): return lax.ppermute(x, axis, [(i, (i + step) % size) for i in range(size)])  33.1 us
    all_to_all x1, waiting for transfers between devices, layer(): lax.all_to_all(partial_value, GRP_TP, split_axis=0, concat_axis=0, tiled=...  26.2 us
    all_to_all x1, waiting for transfers between devices, layer(): lax.all_to_all(outgoing, TP_SEC_GRP, split_axis=0, concat_axis=0, tiled=T...  25.7 us
    all_to_all x1, waiting for transfers between devices, layer(): lax.all_to_all(values.reshape(experts, capacity, width), SEC_GRP, split_a...  24.8 us
    unnamed x25, local copies, waits for them, and re-layouts  20.3 us
    all_to_all x1, waiting for transfers between devices, layer(): lax.all_to_all(products.astype(jnp.bfloat16).reshape(chips, -1, products....  16 us
    all_to_all x1, starting transfers between devices, layer(): lax.all_to_all(outgoing, TP_SEC_GRP, split_axis=0, concat_axis=0, tiled=T...  10.3 us
  transfers between devices with their start and end apart: 23, of which 11 were waited for; matrix products, arithmetic and copies ran while one was open for 17% of the time, Pallas kernels for 0%

commit v1 on v0

--- a/solution.py
+++ b/solution.py
@@ -9,7 +9,6 @@
 SEC_GRP = ("sec", "grp_0", "grp_1")
 TP = ("x", "core")
 GRP_TP = ("grp_0", "grp_1", "x", "core")
-TP_SEC_GRP = ("x", "core", "sec", "grp_0", "grp_1")
 SEC_GRP_TP = ("sec", "grp_0", "grp_1", "x", "core")
 
 
@@ -85,7 +84,8 @@
         product = jnp.dot(
             jnp.concatenate(gathered), out_block, preferred_element_type=jnp.float32
         ).astype(jnp.bfloat16)
-        products.append(product.reshape(len(gathered), 2, rows, columns))
+        product = jnp.pad(product, ((0, 0), (0, -columns % 128)))
+        products.append(product.reshape(len(gathered), 2, rows, -1))
     near, far = products
     places = jnp.concatenate([near[:3], far, near[3:]])
     places = rolled(jnp.moveaxis(places, 1, 0), lax.axis_index("grp_1"))
@@ -140,22 +140,26 @@
     slice_width = expert_in.shape[3]
 
     head_rows = attention_rows(queries, latent_cache, lengths, w_uv)
-    head_rows, expert_in, expert_out = lax.optimization_barrier(
-        (head_rows, expert_in, expert_out)
-    )
+    head_rows, expert_in = lax.optimization_barrier((head_rows, expert_in))
 
     rows_of_chip = width // chips
     in_parts = [
-        lax.dynamic_slice_in_dim(expert_in[0], (chip - step) % chips * rows_of_chip, rows_of_chip, 0)
+        lax.dynamic_slice_in_dim(expert_in[0], (chip + step) % chips * rows_of_chip, rows_of_chip, 0)
         for step in range(chips)
     ]
-    in_parts[1:] = [shifted(in_parts[step], "x", -step) for step in range(1, chips)]
-    out_before, out_after = shifted(expert_out[0], "x", 1), shifted(expert_out[0], "x", -1)
+    in_parts[1:] = [shifted(in_parts[step], "x", step) for step in range(1, chips)]
 
     out_block = attn_weight[:, 0].reshape(-1, attn_weight.shape[3])
     partial_value = projected(head_rows, out_block)
     partial_value = partial_value.reshape(groups * slices, count_of_tokens, -1)
+    partial_value, expert_out = lax.optimization_barrier((partial_value, expert_out))
     arrived = lax.all_to_all(partial_value, GRP_TP, split_axis=0, concat_axis=0, tiled=True)
+    out_parts = [
+        lax.dynamic_slice_in_dim(expert_out[0], (chip + step) % chips * rows_of_chip, rows_of_chip, 1)
+        for step in range(chips)
+    ]
+    out_parts[1:] = [shifted(out_parts[step], "x", step) for step in range(1, chips)]
+    arrived = arrived[:, :, : attn_weight.shape[3]]
     summed = arrived.reshape(groups, slices, count_of_tokens, -1).astype(jnp.float32).sum(axis=1)
     attention = jnp.moveaxis(summed.astype(jnp.bfloat16), 0, 1).reshape(count_of_tokens, width)
 
@@ -186,67 +190,53 @@
     )
     expert_gate = jnp.sum(jnp.where(picked, gate_weights[:, :, None], 0.0), axis=1)
     outgoing = jnp.einsum(
-        "poy,ptj->toyj",
+        "poy,ptj->otyj",
         placed_tokens.astype(jnp.bfloat16),
         normalized_input.reshape(count_of_tokens, slices, part),
         preferred_element_type=jnp.float32,
     ).astype(jnp.bfloat16)
     combine_rows = placed_tokens.astype(jnp.float32) * expert_gate[:, :, None]
-    outgoing = outgoing.reshape(slices * experts, capacity, part)
+    outgoing = outgoing.reshape(experts * slices, capacity, part)
     rows = lax.all_to_all(
-        outgoing, TP_SEC_GRP, split_axis=0, concat_axis=0, tiled=True
+        outgoing, SEC_GRP_TP, split_axis=0, concat_axis=0, tiled=True
     ).reshape(-1, part)
 
-    in_parts, out_before, out_after, _ = lax.optimization_barrier(
-        (in_parts, out_before, out_after, outgoing)
-    )
+    in_parts, out_parts, _ = lax.optimization_barrier((in_parts, out_parts, outgoing))
     in_columns = jnp.concatenate(
         [p.reshape(rows_of_chip, 2 * slice_width) for p in in_parts], axis=1
     )
     in_own, in_other = own_and_other(in_columns, core, 0)
-    middle = slice_width // 2
-    out_opposite = [
-        shifted(out_before[:middle], "x", 1), shifted(out_after[middle:], "x", -1)
-    ]
-    out_own = jnp.concatenate([expert_out[0], out_after, *out_opposite, out_before])
-    out_other = shifted(out_own, "core", 1)
+    out_own, out_sent = own_and_other(jnp.concatenate(out_parts), core, 1)
+    out_other = shifted(out_sent, "core", 1)
 
     other_rows = shifted(rows, "core", 1)
     products = jnp.dot(rows, in_own, preferred_element_type=jnp.float32) + jnp.dot(
         other_rows, in_other, preferred_element_type=jnp.float32
     )
-    gate_up = lax.all_to_all(
-        products.astype(jnp.bfloat16).reshape(chips, -1, products.shape[1]),
-        "x", split_axis=0, concat_axis=0, tiled=True,
-    )
-    parts_of = gate_up.astype(jnp.float32)
-    activated = []
-    for number in range(chips):
-        starts = [(number - p) % chips * 2 * slice_width for p in range(chips)]
-        gate_value, up_value = (
-            sum(
-                parts_of[p, :, start + first : start + first + slice_width]
-                for p, start in enumerate(starts)
-            )
-            for first in (0, slice_width)
-        )
-        activated.append((jax.nn.silu(gate_value) * up_value).astype(jnp.bfloat16))
-    activated = jnp.concatenate(list(rolled(jnp.stack(activated), chips - chip)), axis=1)
-    hidden_own, hidden_sent = own_and_other(activated, core, 0)
-    hidden_other = shifted(hidden_sent, "core", 1)
+    products = jnp.split(products, chips, axis=1)
+    gate_up = products[0]
+    for step in (2, 1, 3):
+        block = shifted(products[step].astype(jnp.bfloat16), "x", -step)
+        gate_up = gate_up + block.astype(jnp.float32)
+    activated = (jax.nn.silu(gate_up[:, :slice_width]) * gate_up[:, slice_width:]).astype(
+        jnp.bfloat16
+    )
+    hidden_own = jnp.concatenate(
+        [activated] + [shifted(activated, "x", step) for step in range(1, chips)], axis=1
+    )
+    hidden_other = shifted(hidden_own, "core", 1)
     values = (
         jnp.dot(hidden_own, out_own, preferred_element_type=jnp.float32)
         + jnp.dot(hidden_other, out_other, preferred_element_type=jnp.float32)
     ).astype(jnp.bfloat16)
     back = lax.all_to_all(
-        values.reshape(experts, capacity, width), SEC_GRP, split_axis=0, concat_axis=0, tiled=True
-    ).reshape(experts * capacity, width)
+        values.reshape(experts * slices, capacity, part),
+        SEC_GRP_TP, split_axis=0, concat_axis=0, tiled=True,
+    ).reshape(experts, slices, capacity, part)
     coarse = lax.reduce_precision(combine_rows, 8, 7)
     weights = jnp.concatenate([coarse, combine_rows - coarse], axis=0).astype(jnp.bfloat16)
-    mixed = jnp.dot(
-        weights.reshape(2 * count_of_tokens, -1), back, preferred_element_type=jnp.float32
-    )
-    expert_mix = mixed[:count_of_tokens] + mixed[count_of_tokens:]
+    mixed = jnp.einsum("poy,otyj->ptj", weights, back, preferred_element_type=jnp.float32)
+    expert_mix = (mixed[:count_of_tokens] + mixed[count_of_tokens:]).reshape(count_of_tokens, width)
     return (residual + expert_mix).astype(jnp.bfloat16)
 
 

time: 276 us -> 240 us (0.87)
  waiting for transfers between devices: 143 us -> 95 us
  starting transfers between devices: 61.2 us -> 81 us
  matrix products: 26.3 us -> 19.1 us
    all_to_all x3 -> x2, waiting for transfers between devices: 66.5 us -> 40.8 us  [the longest x1 27.7 us: layer(): lax.all_to_all(values.reshape(experts * slices, capacity, part), SEC_GRP_...]
    all_to_all x1, waiting for transfers between devices: 26.2 us -> 4.73 us  [layer(): lax.all_to_all(partial_value, GRP_TP, split_axis=0, concat_axis=0, tiled=...]
    all_to_all x3 -> x2, starting transfers between devices: 18.9 us -> 36.8 us  [the longest x1 30.2 us: layer(): lax.all_to_all(outgoing, SEC_GRP_TP, split_axis=0, concat_axis=0, tiled=T...]
    dot_general x1, matrix products: 4.47 us -> 0.71 us  [layer(): jnp.dot(hidden_other, out_other, preferred_element_type=jnp.float32)]
    unnamed x25 -> x29, local copies, waits for them, and re-layouts: 20.3 us -> 17.1 us
    dynamic_slice x1 -> x2, local copies, waits for them, and re-layouts: 4.95 us -> 7.64 us  [the longest x1 5.08 us: layer(): lax.dynamic_slice_in_dim(expert_in[0], (chip + step) % chips * rows_of_ch...]
    ppermute x19 -> x24, starting transfers between devices: 33.1 us -> 35.1 us  [shifted(): return lax.ppermute(x, axis, [(i, (i + step) % size) for i in range(size)])]
    ppermute x19 -> x24, waiting for transfers between devices: 50.7 us -> 49.5 us  [shifted(): return lax.ppermute(x, axis, [(i, (i + step) % size) for i in range(size)])]
  transfers between devices with their start and end apart: 23 -> 27, of which waited for: 11 -> 14; matrix products, arithmetic and copies ran while one was open for 17% -> 17% of each run, Pallas kernels for 0% -> 0%
where the time goes in v1:
time: 240 us; the launch traced here: 238 us
  waiting for transfers between devices  95 us (40%)
  starting transfers between devices  81 us (34%)
  local copies, waits for them, and re-layouts  37.8 us (16%)
  matrix products  19.1 us (8%)
  other arithmetic  3.71 us (2%)
    ppermute x24, waiting for transfers between devices, shifted(): return lax.ppermute(x, axis, [(i, (i + step) % size) for i in range(size)])  49.5 us
    ppermute x24, starting transfers between devices, shifted(): return lax.ppermute(x, axis, [(i, (i + step) % size) for i in range(size)])  35.1 us
    all_to_all x1, starting transfers between devices, layer(): lax.all_to_all(outgoing, SEC_GRP_TP, split_axis=0, concat_axis=0, tiled=T...  30.2 us
    all_to_all x1, waiting for transfers between devices, layer(): lax.all_to_all(values.reshape(experts * slices, capacity, part), SEC_GRP_...  27.7 us
    unnamed x29, local copies, waits for them, and re-layouts  17.1 us
    all_to_all x1, waiting for transfers between devices, layer(): lax.all_to_all(outgoing, SEC_GRP_TP, split_axis=0, concat_axis=0, tiled=T...  13.1 us
    all_to_all x1, starting transfers between devices, layer(): lax.all_to_all(partial_value, GRP_TP, split_axis=0, concat_axis=0, tiled=...  9.15 us
    all_to_all x1, starting transfers between devices, layer(): lax.all_to_all(values.reshape(experts * slices, capacity, part), SEC_GRP_...  6.69 us
  transfers between devices with their start and end apart: 27, of which 14 were waited for; matrix products, arithmetic and copies ran while one was open for 17% of the time, Pallas kernels for 0%

profile of v1, /device:TPU:8, one launch (start us, length us, event | category | flops | bytes accessed | tf_op | source)
XLA Modules:
  0.0 237.7 jit_solution(6468290179798037627)
XLA Ops:
  0.9 2.9 %fusion.30 = f32[32,16,64]{2,1,0:T(8,128)S(1)} fusion(bf16[32,64,576]{2,1,0:T(8,128)(2,1)} %param.14, bf16[32,16,1,576]{3,1,2,0:T(8,128)(2,1)} %param.13, pred[32,64]{1,0:T(8,128)(4,1)S(1)} %iota_compare_fusion.1), kind=kOutput, calls=%fused_computation.25 | convolution fusion | flops 37814272 | bytes 3082240 | tf_op jit(solution)/shard_map/bhr,bpr->bhp/dot_general | solution.py:99
  4.0 2.5 %fusion.19 = bf16[32,16,512]{2,1,0:T(8,128)(2,1)S(1)} fusion(bf16[32,64,576]{2,1,0:T(8,128)(2,1)} %param.14, f32[32,16]{1,0:T(8,128)S(1)} %fusion.74, f32[32,16,64]{2,1,0:T(8,128)S(1)} %fusion.30), kind=kOutput, calls=%fused_computation.19 | convolution fusion | flops 33915456 | bytes 3162112 | tf_op jit(solution)/shard_map/bhp,bpc->bhc/dot_general | solution.py:108
  7.2 2.4 %collective-permute-start = (bf16[32,2048]{1,0:T(8,128)(2,1)S(1)}, bf16[32,2048]{1,0:T(8,128)(2,1)S(1)}, u32[]{:S(2)}, u32[]{:S(2)}) collective-permute-start(bf16[32,2048]{1,0:T(8,128)(2,1)S(1)} %bitcast.111), channel_id=1, source_target_pairs={{0,8},{8,0},{1,9},{9,1},{2,10},{10,2},{3,11},{11,3},{4,12},{12,4},... | collective-permute-start | bytes 393224 | tf_op jit(solution)/shard_map/ppermute | solution.py:21
  10.3 3.8 %collective-permute-done = bf16[32,2048]{1,0:T(8,128)(2,1)S(1)} collective-permute-done((bf16[32,2048]{1,0:T(8,128)(2,1)S(1)}, bf16[32,2048]{1,0:T(8,128)(2,1)S(1)}, u32[]{:S(2)}, u32[]{:S(2)}) %collective-permute-start) | collective-permute-done | bytes 131104 | tf_op jit(solution)/shard_map/ppermute | solution.py:21
  14.7 6.3 %collective-permute-start.2 = (bf16[64,2048]{1,0:T(8,128)(2,1)S(1)}, bf16[64,2048]{1,0:T(8,128)(2,1)S(1)}, u32[]{:S(2)}, u32[]{:S(2)}) collective-permute-start(bf16[64,2048]{1,0:T(8,128)(2,1)S(1)} %get-tuple-element.46), channel_id=1, source_target_pairs={{0,96},{16,112},{32,0},{48,16},{64,32},{80,48},{96,64},{112,80},{1... | collective-permute-start | bytes 786440 | tf_op jit(solution)/shard_map/ppermute | solution.py:21
  21.0 3.7 %collective-permute-start.1 = (bf16[64,2048]{1,0:T(8,128)(2,1)S(1)}, bf16[64,2048]{1,0:T(8,128)(2,1)S(1)}, u32[]{:S(2)}, u32[]{:S(2)}) collective-permute-start(bf16[64,2048]{1,0:T(8,128)(2,1)S(1)} %get-tuple-element.46), channel_id=1, source_target_pairs={{0,112},{16,0},{32,16},{48,32},{64,48},{80,64},{96,80},{112,96},{1... | collective-permute-start | bytes 786440 | tf_op jit(solution)/shard_map/ppermute | solution.py:21
  24.7 3.9 %copy.47 = bf16[16,1,128,448]{2,0,3,1:T(8,128)(2,1)} copy(bf16[16,1,128,448]{2,3,1,0:T(8,128)(2,1)} %param.17) | data formatting | bytes 3670016 | tf_op args[5]
  28.6 3.9 %collective-permute-done.2 = bf16[64,2048]{1,0:T(8,128)(2,1)S(1)} collective-permute-done((bf16[64,2048]{1,0:T(8,128)(2,1)S(1)}, bf16[64,2048]{1,0:T(8,128)(2,1)S(1)}, u32[]{:S(2)}, u32[]{:S(2)}) %collective-permute-start.2) | collective-permute-done | bytes 262176 | tf_op jit(solution)/shard_map/ppermute | solution.py:21
  32.5 4.8 %collective-permute-start.7 = (bf16[32,2048]{1,0:T(8,128)(2,1)S(1)}, bf16[32,2048]{1,0:T(8,128)(2,1)S(1)}, u32[]{:S(2)}, u32[]{:S(2)}) collective-permute-start(bf16[32,2048]{1,0:T(8,128)(2,1)S(1)} %slice.49), channel_id=1, source_target_pairs={{0,96},{16,112},{32,0},{48,16},{64,32},{80,48},{96,64},{112,80},{1... | collective-permute-start | bytes 393224 | tf_op jit(solution)/shard_map/ppermute | solution.py:21
  37.6 2.8 %collective-permute-done.1 = bf16[64,2048]{1,0:T(8,128)(2,1)S(1)} collective-permute-done((bf16[64,2048]{1,0:T(8,128)(2,1)S(1)}, bf16[64,2048]{1,0:T(8,128)(2,1)S(1)}, u32[]{:S(2)}, u32[]{:S(2)}) %collective-permute-start.1) | collective-permute-done | bytes 262176 | tf_op jit(solution)/shard_map/ppermute | solution.py:21
  40.4 2.7 %collective-permute-start.5 = (bf16[64,2048]{1,0:T(8,128)(2,1)S(1)}, bf16[64,2048]{1,0:T(8,128)(2,1)S(1)}, u32[]{:S(2)}, u32[]{:S(2)}) collective-permute-start(bf16[64,2048]{1,0:T(8,128)(2,1)S(1)} %collective-permute-done.2), channel_id=1, source_target_pairs={{0,112},{16,0},{32,16},{48,32},{64,48},{80,64},{96,80},{112,96},{1... | collective-permute-start | bytes 786440 | tf_op jit(solution)/shard_map/ppermute | solution.py:21
  46.0 2.2 fusion.22
  48.2 3.8 %collective-permute-done.8 = bf16[64,2048]{1,0:T(8,128)(2,1)S(1)} collective-permute-done((bf16[64,2048]{1,0:T(8,128)(2,1)S(1)}, bf16[64,2048]{1,0:T(8,128)(2,1)S(1)}, u32[]{:S(2)}, u32[]{:S(2)}) %collective-permute-start.8) | collective-permute-done | bytes 262176 | tf_op jit(solution)/shard_map/ppermute | solution.py:21
  54.2 9.1 %all-to-all-start = ((bf16[128,4,512]{2,1,0:T(4,128)(2,1)}), bf16[128,4,512]{2,1,0:T(4,128)(2,1)S(1)}, u32[]{:S(2)}, u32[]{:S(2)}) async-start(bf16[128,4,512]{2,1,0:T(4,128)(2,1)} %reshape.192), calls=%async_computation | async-start | bytes 1048576 | tf_op jit(solution)/shard_map/all_to_all | solution.py:156
  63.4 5.1 %dynamic-slice_bitcast_fusion = (bf16[1792,2,128]{2,1,0:T(2,128)(2,1)}, bf16[1792,2,128]{2,1,0:T(2,128)(2,1)}, bf16[1792,2,128]{2,1,0:T(2,128)(2,1)}, bf16[1792,2,128]{2,1,0:T(2,128)(2,1)}) fusion(bf16[1,7168,2,128]{3,2,1,0:T(2,128)(2,1)} %param.22, s32[]{:T(128)S(6)} %select_n.81, s32[]{:T(128)S(6)} %select_n.79, s32[]{:T(128)S(6)} %select_n.77, ...), kind=kLoop, calls=%fused_computation.44 | loop fusion | bytes 7340048 | tf_op jit(solution)/shard_map/dynamic_slice | solution.py:147
  68.4 1.1 collective-permute-start.9
  69.6 2.7 %collective-permute-start.10 = (bf16[1792,2,128]{2,1,0:T(2,128)(2,1)}, bf16[1792,2,128]{2,1,0:T(2,128)(2,1)}, u32[]{:S(2)}, u32[]{:S(2)}) collective-permute-start(bf16[1792,2,128]{2,1,0:T(2,128)(2,1)} %get-tuple-element.36), channel_id=1, source_target_pairs={{0,4},{2,6},{4,0},{6,2},{1,5},{3,7},{5,1},{7,3},{8,12},{10,14},{12... | collective-permute-start | bytes 2752520 | tf_op jit(solution)/shard_map/ppermute | solution.py:21
  72.3 1.5 collective-permute-start.11
  74.6 2.6 %dynamic-slice_bitcast_fusion.4 = (bf16[128,1792]{1,0:T(8,128)(2,1)}, bf16[128,1792]{1,0:T(8,128)(2,1)}, bf16[128,1792]{1,0:T(8,128)(2,1)}, bf16[128,1792]{1,0:T(8,128)(2,1)S(1)}) fusion(bf16[1,128,7168]{2,1,0:T(8,128)(2,1)} %param.23, s32[]{:T(128)S(6)} %select_n.81, s32[]{:T(128)S(6)} %select_n.79, s32[]{:T(128)S(6)} %select_n.77, s32[]{:T(128)S(6)} %select_n.75), kind=kLoop, calls=%fused_computation.66 | loop fusion | bytes 3670032 | tf_op jit(solution)/shard_map/dynamic_slice | solution.py:158
  78.6 4.7 %all-to-all-done = bf16[128,4,512]{2,1,0:T(4,128)(2,1)S(1)} async-done(((bf16[128,4,512]{2,1,0:T(4,128)(2,1)}), bf16[128,4,512]{2,1,0:T(4,128)(2,1)S(1)}, u32[]{:S(2)}, u32[]{:S(2)}) %all-to-all-start) | async-done | bytes 524320 | tf_op jit(solution)/shard_map/all_to_all | solution.py:156
  84.1 1.2 fusion.39
  85.7 10.6 %collective-permute-done.9 = bf16[1792,2,128]{2,1,0:T(2,128)(2,1)} collective-permute-done((bf16[1792,2,128]{2,1,0:T(2,128)(2,1)}, bf16[1792,2,128]{2,1,0:T(2,128)(2,1)}, u32[]{:S(2)}, u32[]{:S(2)}) %collective-permute-start.9) | collective-permute-done | bytes 917536 | tf_op jit(solution)/shard_map/ppermute | solution.py:21
  97.8 2.0 copy.51
  99.8 30.2 %all-to-all-start.1 = ((bf16[256,2,896]{2,1,0:T(2,128)(2,1)}), bf16[256,2,896]{2,1,0:T(2,128)(2,1)S(1)}, u32[]{:S(2)}, u32[]{:S(2)}) async-start(bf16[256,2,896]{2,1,0:T(2,128)(2,1)} %copy.51), calls=%async_computation.1 | async-start | bytes 1835008 | tf_op jit(solution)/shard_map/all_to_all | solution.py:200
  130.0 6.1 %collective-permute-done.13 = bf16[128,1792]{1,0:T(8,128)(2,1)} collective-permute-done((bf16[128,1792]{1,0:T(8,128)(2,1)}, bf16[128,1792]{1,0:T(8,128)(2,1)}, u32[]{:S(2)}, u32[]{:S(2)}) %collective-permute-start.13) | collective-permute-done | bytes 458784 | tf_op jit(solution)/shard_map/ppermute | solution.py:21
  137.0 1.8 constant_dynamic-update-slice_fusion.10
  138.8 1.2 bitcast_dynamic-update-slice_fusion.3
  140.0 2.3 bitcast_dynamic-update-slice_fusion.2
  142.3 2.3 bitcast_dynamic-update-slice_fusion.1
  144.6 13.1 %all-to-all-done.1 = bf16[256,2,896]{2,1,0:T(2,128)(2,1)S(1)} async-done(((bf16[256,2,896]{2,1,0:T(2,128)(2,1)}), bf16[256,2,896]{2,1,0:T(2,128)(2,1)S(1)}, u32[]{:S(2)}, u32[]{:S(2)}) %all-to-all-start.1) | async-done | bytes 917536 | tf_op jit(solution)/shard_map/all_to_all | solution.py:200
  157.7 1.3 reshape.196
  158.9 1.9 constant_dynamic-update-slice_fusion.9
  160.8 2.3 bitcast_dynamic-update-slice_fusion
  163.1 2.8 %fusion.11 = f32[512,1024]{1,0:T(8,128)S(1)} fusion(bf16[512,896]{1,0:T(8,128)(2,1)S(1)} %copy-done.5, bf16[1792,1024]{1,0:T(8,128)(2,1)} %bitcast_dynamic-update-slice_fusion, s32[]{:T(128)S(6)} %select_n.82), kind=kOutput, calls=%fused_computation.12 | convolution fusion | flops 939524096 | bytes 4849668 | tf_op jit(solution)/shard_map/dot_general | solution.py:213
  165.9 2.8 %fusion.75 = (bf16[512,1024]{1,0:T(8,128)(2,1)S(1)}, f32[512,1024]{1,0:T(8,128)S(1)}) fusion(f32[512,1024]{1,0:T(8,128)S(1)} %fusion.11, bf16[512,896]{1,0:T(8,128)(2,1)S(1)} %collective-permute-done.15, bf16[1792,1024]{1,0:T(8,128)(2,1)} %bitcast_dynamic-update-slice_fusion, s32[]{:T(128)S(6)} %select_n.83), kind=kOutput, calls=%fused_computation.126 | convolution fusion | flops 940572672 | bytes 7995396 | tf_op jit(solution)/shard_map/dot_general | solution.py:213
  169.4 2.7 %collective-permute-start.17 = (bf16[512,256]{1,0:T(8,128)(2,1)S(1)}, bf16[512,256]{1,0:T(8,128)(2,1)S(1)}, u32[]{:S(2)}, u32[]{:S(2)}) collective-permute-start(bf16[512,256]{1,0:T(8,128)(2,1)S(1)} %get-tuple-element.45), channel_id=1, source_target_pairs={{0,6},{2,0},{4,2},{6,4},{1,7},{3,1},{5,3},{7,5},{8,14},{10,8},{12,... | collective-permute-start | bytes 786440 | tf_op jit(solution)/shard_map/ppermute | solution.py:21
  172.1 1.8 constant_dynamic-update-slice_fusion.8
  174.0 1.3 constant_dynamic-slice_fusion
  175.3 9.0 %collective-permute-done.18 = bf16[512,256]{1,0:T(8,128)(2,1)S(1)} collective-permute-done((bf16[512,256]{1,0:T(8,128)(2,1)S(1)}, bf16[512,256]{1,0:T(8,128)(2,1)S(1)}, u32[]{:S(2)}, u32[]{:S(2)}) %collective-permute-start.18) | collective-permute-done | bytes 262176 | tf_op jit(solution)/shard_map/ppermute | solution.py:21
  184.6 3.0 %collective-permute-start.21 = (bf16[512,128]{1,0:T(8,128)(2,1)S(1)}, bf16[512,128]{1,0:T(8,128)(2,1)S(1)}, u32[]{:S(2)}, u32[]{:S(2)}) collective-permute-start(bf16[512,128]{1,0:T(8,128)(2,1)S(1)} %fusion.56), channel_id=1, source_target_pairs={{0,6},{2,0},{4,2},{6,4},{1,7},{3,1},{5,3},{7,5},{8,14},{10,8},{12,... | collective-permute-start | bytes 393224 | tf_op jit(solution)/shard_map/ppermute | solution.py:21
  188.6 4.1 %collective-permute-done.21 = bf16[512,128]{1,0:T(8,128)(2,1)S(1)} collective-permute-done((bf16[512,128]{1,0:T(8,128)(2,1)S(1)}, bf16[512,128]{1,0:T(8,128)(2,1)S(1)}, u32[]{:S(2)}, u32[]{:S(2)}) %collective-permute-start.21) | collective-permute-done | bytes 131104 | tf_op jit(solution)/shard_map/ppermute | solution.py:21
  192.7 2.3 collective-permute-done.20
  195.0 1.1 collective-permute-done.19
  196.5 1.9 collective-permute-done.22
  199.1 1.9 add_convert_fusion
  201.0 1.3 reshape.201
  202.3 6.7 %all-to-all-start.2 = ((bf16[256,2,896]{2,1,0:T(2,128)(2,1)}), bf16[256,2,896]{2,1,0:T(2,128)(2,1)S(1)}, u32[]{:S(2)}, u32[]{:S(2)}) async-start(bf16[256,2,896]{2,1,0:T(2,128)(2,1)} %reshape.201), calls=%async_computation.2 | async-start | bytes 1835008 | tf_op jit(solution)/shard_map/all_to_all | solution.py:232
  209.0 27.7 %all-to-all-done.2 = bf16[256,2,896]{2,1,0:T(2,128)(2,1)S(1)} async-done(((bf16[256,2,896]{2,1,0:T(2,128)(2,1)}), bf16[256,2,896]{2,1,0:T(2,128)(2,1)S(1)}, u32[]{:S(2)}, u32[]{:S(2)}) %all-to-all-start.2) | async-done | bytes 917536 | tf_op jit(solution)/shard_map/all_to_all | solution.py:232
  (93 shorter events, 17.5 us)
Async XLA Ops:
  0.0 6.5 %copy-start = (bf16[16,1,512,128]{3,2,1,0:T(8,128)(2,1)S(1)}, bf16[16,1,512,128]{3,2,1,0:T(8,128)(2,1)}, u32[]{:S(2)}) copy-start(bf16[16,1,512,128]{3,2,1,0:T(8,128)(2,1)} %param.16) | copy-start | bytes 6291460
  7.2 6.8 %collective-permute-start = (bf16[32,2048]{1,0:T(8,128)(2,1)S(1)}, bf16[32,2048]{1,0:T(8,128)(2,1)S(1)}, u32[]{:S(2)}, u32[]{:S(2)}) collective-permute-start(bf16[32,2048]{1,0:T(8,128)(2,1)S(1)} %bitcast.111), channel_id=1, source_target_pairs={{0,8},{8,0},{1,9},{9,1},{2,10},{10,2},{3,11},{11,3},{4,12},{12,4},... | collective-permute-start | bytes 393224 | tf_op jit(solution)/shard_map/ppermute | solution.py:21
  14.7 17.8 %collective-permute-start.2 = (bf16[64,2048]{1,0:T(8,128)(2,1)S(1)}, bf16[64,2048]{1,0:T(8,128)(2,1)S(1)}, u32[]{:S(2)}, u32[]{:S(2)}) collective-permute-start(bf16[64,2048]{1,0:T(8,128)(2,1)S(1)} %get-tuple-element.46), channel_id=1, source_target_pairs={{0,96},{16,112},{32,0},{48,16},{64,32},{80,48},{96,64},{112,80},{1... | collective-permute-start | bytes 786440 | tf_op jit(solution)/shard_map/ppermute | solution.py:21
  21.0 16.3 %collective-permute-start.3 = (bf16[64,2048]{1,0:T(8,128)(2,1)S(1)}, bf16[64,2048]{1,0:T(8,128)(2,1)S(1)}, u32[]{:S(2)}, u32[]{:S(2)}) collective-permute-start(bf16[64,2048]{1,0:T(8,128)(2,1)S(1)} %get-tuple-element.46), channel_id=1, source_target_pairs={{0,32},{16,48},{32,64},{48,80},{64,96},{80,112},{96,0},{112,16},{1... | collective-permute-start | bytes 786440 | tf_op jit(solution)/shard_map/ppermute | solution.py:21
  21.0 19.4 %collective-permute-start.1 = (bf16[64,2048]{1,0:T(8,128)(2,1)S(1)}, bf16[64,2048]{1,0:T(8,128)(2,1)S(1)}, u32[]{:S(2)}, u32[]{:S(2)}) collective-permute-start(bf16[64,2048]{1,0:T(8,128)(2,1)S(1)} %get-tuple-element.46), channel_id=1, source_target_pairs={{0,112},{16,0},{32,16},{48,32},{64,48},{80,64},{96,80},{112,96},{1... | collective-permute-start | bytes 786440 | tf_op jit(solution)/shard_map/ppermute | solution.py:21
  28.6 17.3 %copy-start.2 = (bf16[16,1,128,448]{2,0,3,1:T(8,128)(2,1)S(1)}, bf16[16,1,128,448]{2,0,3,1:T(8,128)(2,1)}, u32[]{:S(2)}) copy-start(bf16[16,1,128,448]{2,0,3,1:T(8,128)(2,1)} %copy.47) | copy-start | bytes 5505028
  28.6 16.6 %collective-permute-start.4 = (bf16[64,2048]{1,0:T(8,128)(2,1)S(1)}, bf16[64,2048]{1,0:T(8,128)(2,1)S(1)}, u32[]{:S(2)}, u32[]{:S(2)}) collective-permute-start(bf16[64,2048]{1,0:T(8,128)(2,1)S(1)} %get-tuple-element.46), channel_id=1, source_target_pairs={{0,16},{16,32},{32,48},{48,64},{64,80},{80,96},{96,112},{112,0},{1... | collective-permute-start | bytes 786440 | tf_op jit(solution)/shard_map/ppermute | solution.py:21
  32.5 15.7 %collective-permute-start.7 = (bf16[32,2048]{1,0:T(8,128)(2,1)S(1)}, bf16[32,2048]{1,0:T(8,128)(2,1)S(1)}, u32[]{:S(2)}, u32[]{:S(2)}) collective-permute-start(bf16[32,2048]{1,0:T(8,128)(2,1)S(1)} %slice.49), channel_id=1, source_target_pairs={{0,96},{16,112},{32,0},{48,16},{64,32},{80,48},{96,64},{112,80},{1... | collective-permute-start | bytes 393224 | tf_op jit(solution)/shard_map/ppermute | solution.py:21
  37.3 10.9 %collective-permute-start.6 = (bf16[32,2048]{1,0:T(8,128)(2,1)S(1)}, bf16[32,2048]{1,0:T(8,128)(2,1)S(1)}, u32[]{:S(2)}, u32[]{:S(2)}) collective-permute-start(bf16[32,2048]{1,0:T(8,128)(2,1)S(1)} %slice.48), channel_id=1, source_target_pairs={{0,32},{16,48},{32,64},{48,80},{64,96},{80,112},{96,0},{112,16},{1... | collective-permute-start | bytes 393224 | tf_op jit(solution)/shard_map/ppermute | solution.py:21
  37.4 14.6 %collective-permute-start.8 = (bf16[64,2048]{1,0:T(8,128)(2,1)S(1)}, bf16[64,2048]{1,0:T(8,128)(2,1)S(1)}, u32[]{:S(2)}, u32[]{:S(2)}) collective-permute-start(bf16[64,2048]{1,0:T(8,128)(2,1)S(1)} %collective-permute-done.3), channel_id=1, source_target_pairs={{0,16},{16,32},{32,48},{48,64},{64,80},{80,96},{96,112},{112,0},{1... | collective-permute-start | bytes 786440 | tf_op jit(solution)/shard_map/ppermute | solution.py:21
  40.4 11.7 %collective-permute-start.5 = (bf16[64,2048]{1,0:T(8,128)(2,1)S(1)}, bf16[64,2048]{1,0:T(8,128)(2,1)S(1)}, u32[]{:S(2)}, u32[]{:S(2)}) collective-permute-start(bf16[64,2048]{1,0:T(8,128)(2,1)S(1)} %collective-permute-done.2), channel_id=1, source_target_pairs={{0,112},{16,0},{32,16},{48,32},{64,48},{80,64},{96,80},{112,96},{1... | collective-permute-start | bytes 786440 | tf_op jit(solution)/shard_map/ppermute | solution.py:21
  54.2 29.2 %all-to-all-start = ((bf16[128,4,512]{2,1,0:T(4,128)(2,1)}), bf16[128,4,512]{2,1,0:T(4,128)(2,1)S(1)}, u32[]{:S(2)}, u32[]{:S(2)}) async-start(bf16[128,4,512]{2,1,0:T(4,128)(2,1)} %reshape.192), calls=%async_computation | async-start | bytes 1048576 | tf_op jit(solution)/shard_map/all_to_all | solution.py:156
  63.4 11.0 %copy-start.8 = (s32[4,8]{1,0:T(4,128)S(1)}, s32[4,8]{1,0:T(4,128)}, u32[]{:S(2)}) copy-start(s32[4,8]{1,0:T(4,128)} %param.20) | copy-start | bytes 388
  68.4 27.9 %collective-permute-start.9 = (bf16[1792,2,128]{2,1,0:T(2,128)(2,1)}, bf16[1792,2,128]{2,1,0:T(2,128)(2,1)}, u32[]{:S(2)}, u32[]{:S(2)}) collective-permute-start(bf16[1792,2,128]{2,1,0:T(2,128)(2,1)} %get-tuple-element.37), channel_id=1, source_target_pairs={{0,2},{2,4},{4,6},{6,0},{1,3},{3,5},{5,7},{7,1},{8,10},{10,12},{12... | collective-permute-start | bytes 2752520 | tf_op jit(solution)/shard_map/ppermute | solution.py:21
  69.6 60.4 %collective-permute-start.10 = (bf16[1792,2,128]{2,1,0:T(2,128)(2,1)}, bf16[1792,2,128]{2,1,0:T(2,128)(2,1)}, u32[]{:S(2)}, u32[]{:S(2)}) collective-permute-start(bf16[1792,2,128]{2,1,0:T(2,128)(2,1)} %get-tuple-element.36), channel_id=1, source_target_pairs={{0,4},{2,6},{4,0},{6,2},{1,5},{3,7},{5,1},{7,3},{8,12},{10,14},{12... | collective-permute-start | bytes 2752520 | tf_op jit(solution)/shard_map/ppermute | solution.py:21
  72.3 57.7 %collective-permute-start.11 = (bf16[1792,2,128]{2,1,0:T(2,128)(2,1)}, bf16[1792,2,128]{2,1,0:T(2,128)(2,1)}, u32[]{:S(2)}, u32[]{:S(2)}) collective-permute-start(bf16[1792,2,128]{2,1,0:T(2,128)(2,1)} %get-tuple-element.35), channel_id=1, source_target_pairs={{0,6},{2,0},{4,2},{6,4},{1,7},{3,1},{5,3},{7,5},{8,14},{10,8},{12,... | collective-permute-start | bytes 2752520 | tf_op jit(solution)/shard_map/ppermute | solution.py:21
  74.6 9.2 %copy-start.6 = (bf16[4,7168]{1,0:T(4,128)(2,1)S(1)}, bf16[4,7168]{1,0:T(4,128)(2,1)}, u32[]{:S(2)}) copy-start(bf16[4,7168]{1,0:T(4,128)(2,1)} %param.12) | copy-start | bytes 172036
  74.6 9.4 %copy-start.7 = (f32[7168]{0:T(1024)S(1)}, f32[7168]{0:T(1024)}, u32[]{:S(2)}) copy-start(f32[7168]{0:T(1024)} %param.18) | copy-start | bytes 86020
  77.2 52.8 %collective-permute-start.12 = (bf16[128,1792]{1,0:T(8,128)(2,1)}, bf16[128,1792]{1,0:T(8,128)(2,1)}, u32[]{:S(2)}, u32[]{:S(2)}) collective-permute-start(bf16[128,1792]{1,0:T(8,128)(2,1)} %get-tuple-element.41), channel_id=1, source_target_pairs={{0,2},{2,4},{4,6},{6,0},{1,3},{3,5},{5,7},{7,1},{8,10},{10,12},{12... | collective-permute-start | bytes 1376264 | tf_op jit(solution)/shard_map/ppermute | solution.py:21
  77.7 58.4 %collective-permute-start.13 = (bf16[128,1792]{1,0:T(8,128)(2,1)}, bf16[128,1792]{1,0:T(8,128)(2,1)}, u32[]{:S(2)}, u32[]{:S(2)}) collective-permute-start(bf16[128,1792]{1,0:T(8,128)(2,1)} %get-tuple-element.40), channel_id=1, source_target_pairs={{0,4},{2,6},{4,0},{6,2},{1,5},{3,7},{5,1},{7,3},{8,12},{10,14},{12... | collective-permute-start | bytes 1376264 | tf_op jit(solution)/shard_map/ppermute | solution.py:21
  83.8 14.0 %copy-start.3 = (f32[4,7168]{1,0:T(4,128)}, f32[4,7168]{1,0:T(4,128)S(1)}, u32[]{:S(2)}) copy-start(f32[4,7168]{1,0:T(4,128)S(1)} %reshape.204) | copy-start | bytes 344068
  96.4 39.8 %collective-permute-start.14 = (bf16[128,1792]{1,0:T(8,128)(2,1)}, bf16[128,1792]{1,0:T(8,128)(2,1)}, u32[]{:S(2)}, u32[]{:S(2)}) collective-permute-start(bf16[128,1792]{1,0:T(8,128)(2,1)} %get-tuple-element.39), channel_id=1, source_target_pairs={{0,6},{2,0},{4,2},{6,4},{1,7},{3,1},{5,3},{7,5},{8,14},{10,8},{12,... | collective-permute-start | bytes 1376264 | tf_op jit(solution)/shard_map/ppermute | solution.py:21
  99.8 57.9 %all-to-all-start.1 = ((bf16[256,2,896]{2,1,0:T(2,128)(2,1)}), bf16[256,2,896]{2,1,0:T(2,128)(2,1)S(1)}, u32[]{:S(2)}, u32[]{:S(2)}) async-start(bf16[256,2,896]{2,1,0:T(2,128)(2,1)} %copy.51), calls=%async_computation.1 | async-start | bytes 1835008 | tf_op jit(solution)/shard_map/all_to_all | solution.py:200
  130.0 8.8 %copy-start.1 = (bf16[1792,2,128]{2,1,0:T(2,128)(2,1)S(1)}, bf16[1792,2,128]{2,1,0:T(2,128)(2,1)}, u32[]{:S(2)}) copy-start(bf16[1792,2,128]{2,1,0:T(2,128)(2,1)} %get-tuple-element.21) | copy-start | bytes 2752516
  158.9 4.2 %copy-start.5 = (bf16[512,896]{1,0:T(8,128)(2,1)S(1)}, bf16[512,896]{1,0:T(8,128)(2,1)}, u32[]{:S(2)}) copy-start(bf16[512,896]{1,0:T(8,128)(2,1)} %reshape.196) | copy-start | bytes 2752516
  158.9 7.0 %collective-permute-start.15 = (bf16[512,896]{1,0:T(8,128)(2,1)}, bf16[512,896]{1,0:T(8,128)(2,1)S(1)}, u32[]{:S(2)}, u32[]{:S(2)}) collective-permute-start(bf16[512,896]{1,0:T(8,128)(2,1)} %reshape.196), channel_id=1, source_target_pairs={{0,1},{1,0},{2,3},{3,2},{4,5},{5,4},{6,7},{7,6},{8,9},{9,8},{10,11... | collective-permute-start | bytes 2752520 | tf_op jit(solution)/shard_map/ppermute | solution.py:21
  168.8 15.5 %collective-permute-start.18 = (bf16[512,256]{1,0:T(8,128)(2,1)S(1)}, bf16[512,256]{1,0:T(8,128)(2,1)S(1)}, u32[]{:S(2)}, u32[]{:S(2)}) collective-permute-start(bf16[512,256]{1,0:T(8,128)(2,1)S(1)} %get-tuple-element.44), channel_id=1, source_target_pairs={{0,2},{2,4},{4,6},{6,0},{1,3},{3,5},{5,7},{7,1},{8,10},{10,12},{12... | collective-permute-start | bytes 786440 | tf_op jit(solution)/shard_map/ppermute | solution.py:21
  169.4 15.0 %collective-permute-start.17 = (bf16[512,256]{1,0:T(8,128)(2,1)S(1)}, bf16[512,256]{1,0:T(8,128)(2,1)S(1)}, u32[]{:S(2)}, u32[]{:S(2)}) collective-permute-start(bf16[512,256]{1,0:T(8,128)(2,1)S(1)} %get-tuple-element.45), channel_id=1, source_target_pairs={{0,6},{2,0},{4,2},{6,4},{1,7},{3,1},{5,3},{7,5},{8,14},{10,8},{12,... | collective-permute-start | bytes 786440 | tf_op jit(solution)/shard_map/ppermute | solution.py:21
  172.1 12.2 %collective-permute-start.16 = (bf16[512,256]{1,0:T(8,128)(2,1)S(1)}, bf16[512,256]{1,0:T(8,128)(2,1)S(1)}, u32[]{:S(2)}, u32[]{:S(2)}) collective-permute-start(bf16[512,256]{1,0:T(8,128)(2,1)S(1)} %get-tuple-element.43), channel_id=1, source_target_pairs={{0,4},{2,6},{4,0},{6,2},{1,5},{3,7},{5,1},{7,3},{8,12},{10,14},{12... | collective-permute-start | bytes 786440 | tf_op jit(solution)/shard_map/ppermute | solution.py:21
  175.2 21.3 %collective-permute-start.23 = (bf16[512,896]{1,0:T(8,128)(2,1)S(1)}, bf16[512,896]{1,0:T(8,128)(2,1)S(1)}, u32[]{:S(2)}, u32[]{:S(2)}) collective-permute-start(bf16[512,896]{1,0:T(8,128)(2,1)S(1)} %constant_dynamic-slice_fusion), channel_id=1, source_target_pairs={{0,1},{1,0},{2,3},{3,2},{4,5},{5,4},{6,7},{7,6},{8,9},{9,8},{10,11... | collective-permute-start | bytes 2752520 | tf_op jit(solution)/shard_map/ppermute | solution.py:21
  184.6 8.1 %collective-permute-start.21 = (bf16[512,128]{1,0:T(8,128)(2,1)S(1)}, bf16[512,128]{1,0:T(8,128)(2,1)S(1)}, u32[]{:S(2)}, u32[]{:S(2)}) collective-permute-start(bf16[512,128]{1,0:T(8,128)(2,1)S(1)} %fusion.56), channel_id=1, source_target_pairs={{0,6},{2,0},{4,2},{6,4},{1,7},{3,1},{5,3},{7,5},{8,14},{10,8},{12,... | collective-permute-start | bytes 393224 | tf_op jit(solution)/shard_map/ppermute | solution.py:21
  187.6 7.4 %collective-permute-start.20 = (bf16[512,128]{1,0:T(8,128)(2,1)S(1)}, bf16[512,128]{1,0:T(8,128)(2,1)S(1)}, u32[]{:S(2)}, u32[]{:S(2)}) collective-permute-start(bf16[512,128]{1,0:T(8,128)(2,1)S(1)} %fusion.56), channel_id=1, source_target_pairs={{0,4},{2,6},{4,0},{6,2},{1,5},{3,7},{5,1},{7,3},{8,12},{10,14},{12... | collective-permute-start | bytes 393224 | tf_op jit(solution)/shard_map/ppermute | solution.py:21
  187.6 8.4 %collective-permute-start.19 = (bf16[512,128]{1,0:T(8,128)(2,1)S(1)}, bf16[512,128]{1,0:T(8,128)(2,1)S(1)}, u32[]{:S(2)}, u32[]{:S(2)}) collective-permute-start(bf16[512,128]{1,0:T(8,128)(2,1)S(1)} %fusion.56), channel_id=1, source_target_pairs={{0,2},{2,4},{4,6},{6,0},{1,3},{3,5},{5,7},{7,1},{8,10},{10,12},{12... | collective-permute-start | bytes 393224 | tf_op jit(solution)/shard_map/ppermute | solution.py:21
  196.1 2.3 collective-permute-start.22
  202.3 34.8 %copy-start.4 = (f32[4,7168]{1,0:T(4,128)S(1)}, f32[4,7168]{1,0:T(4,128)}, u32[]{:S(2)}) copy-start(f32[4,7168]{1,0:T(4,128)} %copy-done.3) | copy-start | bytes 344068
  202.3 34.4 %all-to-all-start.2 = ((bf16[256,2,896]{2,1,0:T(2,128)(2,1)}), bf16[256,2,896]{2,1,0:T(2,128)(2,1)S(1)}, u32[]{:S(2)}, u32[]{:S(2)}) async-start(bf16[256,2,896]{2,1,0:T(2,128)(2,1)} %reshape.201), calls=%async_computation.2 | async-start | bytes 1835008 | tf_op jit(solution)/shard_map/all_to_all | solution.py:232
